TPU v7x, 256 devices: a whole 4x4x8 slice. The times are simulated.
256 devices in a mesh: wide: 16 (over y, z_hi), narrow: 16 (over x, z_lo, core).
Axes of the slice: x: 4, y: 4, z: 8 (z_hi: 4, z_lo: 2; z = z_hi * 2 + z_lo), core: 2. Of those that a mesh axis runs over, the one named last changes fastest.
Arguments:
- features: bfloat16 [65536, 768], P(('wide', 'narrow'))
- proj_weight: bfloat16 [768, 512], replicated, may hold values from -0.21875 to 0.21875
- bias: float32 [512], replicated, may hold values from -1.5 to 1.5
- disc_weight: float32 [512, 512], replicated, may hold values from -0.25 to 0.25
- adjacency: int32 [16, 16, 24, 256, 256], P('wide', 'narrow'), may hold values from 0 to 3
- row_block: int32 [16, 16, 24], P('wide', 'narrow'), may hold values from 0 to 15
- col_block: int32 [16, 16, 24], P('wide', 'narrow'), may hold values from 0 to 15
- block_count: int32 [16, 16], P('wide', 'narrow'), may hold values from 1 to 24, as said below
- degree: int32 [65536], replicated, may hold values from 6 to 65
- corrupt_source: int32 [256], replicated, may hold values from 0 to 255, as said below
Outputs:
- hidden: bfloat16 [65536, 512], P(('wide', 'narrow'))
- scores: float32 [2, 65536], P(None, ('wide', 'narrow'))
- loss: float32 [], replicated
Inputs may be any that keep to these rules, and one draw needn't show every extreme that they name: Only slots below block_count of a tile take part; some tile holds 24 live slots in every draw. corrupt_source is a permutation of the blocks, and block g and block corrupt_source[g] have equal g % 16.
All inputs are finite; a program needn't handle non-finite values.
Results may differ from a plain program's by a relative error of at most 0.0056.
Values may be sent and summed in bfloat16 or wider, within the bound.
No kernel may reach another device: no remote copies, remote signals or barrier semaphores. Data moves between devices by JAX's collectives and lax.ppermute only.
A program may use at most 128 MiB of HBM per device.

v0:
```python
import jax
import jax.numpy as jnp
from jax import lax
from jax.sharding import PartitionSpec as P


def shards(
    features,
    proj_weight,
    bias,
    disc_weight,
    adjacency,
    row_block,
    col_block,
    block_count,
    degree,
    corrupt_source,
):
    rows_dev = features.shape[0]
    block_len = adjacency.shape[-1]
    blocks_dev = rows_dev // block_len
    hidden_width = proj_weight.shape[1]
    wide_size = lax.axis_size("wide")
    narrow_size = lax.axis_size("narrow")
    wide_at = lax.axis_index("wide")
    narrow_at = lax.axis_index("narrow")
    tile_height = blocks_dev * narrow_size
    tile_width = blocks_dev * wide_size
    panel = jnp.dot(
        lax.all_gather(features, "wide", axis=0, tiled=True),
        proj_weight,
        preferred_element_type=jnp.float32,
    ).astype(jnp.bfloat16)
    clean_blocks = panel.reshape(tile_width, block_len, hidden_width)
    local_cols = jnp.arange(tile_width, dtype=jnp.int32)
    global_cols = (
        local_cols // blocks_dev * narrow_size + narrow_at
    ) * blocks_dev + local_cols % blocks_dev
    sources = jnp.take(corrupt_source, global_cols)
    source_local = sources // blocks_dev // narrow_size * blocks_dev + sources % blocks_dev
    corrupt_blocks = jnp.take(clean_blocks, source_local, axis=0)
    inv_root = lax.rsqrt(degree.astype(jnp.float32))
    col_roots = lax.dynamic_index_in_dim(
        inv_root.reshape(wide_size, narrow_size, rows_dev), narrow_at, 1, keepdims=False
    )
    row_roots = lax.dynamic_index_in_dim(
        inv_root.reshape(wide_size, tile_height, block_len), wide_at, 0, keepdims=False
    )
    slot_rows = row_block[0, 0]
    slot_cols = col_block[0, 0]
    normed = (
        adjacency[0, 0].astype(jnp.float32)
        * row_roots[slot_rows][:, :, None]
        * col_roots[slot_cols][:, None, :]
    ).astype(jnp.bfloat16)
    live_slots = block_count[0, 0]
    joined = jnp.concatenate((clean_blocks, corrupt_blocks), axis=2)
    width = joined.shape[2]

    def add_slot(slot, totals):
        term = jnp.dot(normed[slot], joined[slot_cols[slot]], preferred_element_type=jnp.float32)
        return totals.at[slot_rows[slot]].add(term)

    totals = lax.fori_loop(
        jnp.int32(0), live_slots, add_slot, jnp.zeros((tile_height, block_len, width), jnp.float32)
    )
    summed = lax.psum_scatter(
        totals.reshape(tile_height * block_len, width), "narrow", scatter_dimension=0, tiled=True
    )
    clean_sum = summed[:, :hidden_width]
    corrupt_sum = summed[:, hidden_width:]
    own_clean = lax.dynamic_slice_in_dim(clean_blocks, wide_at * blocks_dev, blocks_dev, 0).reshape(
        rows_dev, hidden_width
    )
    own_corrupt = lax.dynamic_slice_in_dim(
        corrupt_blocks, wide_at * blocks_dev, blocks_dev, 0
    ).reshape(rows_dev, hidden_width)
    own_degree = lax.dynamic_index_in_dim(
        degree.reshape(wide_size * narrow_size, rows_dev),
        wide_at * narrow_size + narrow_at,
        0,
        keepdims=False,
    )
    degree_float = own_degree.astype(jnp.float32)[:, None]
    clean_h = jnp.maximum(clean_sum + own_clean.astype(jnp.float32) / degree_float + bias, 0.0)
    corrupt_h = jnp.maximum(
        corrupt_sum + own_corrupt.astype(jnp.float32) / degree_float + bias, 0.0
    )
    node_total = rows_dev * wide_size * narrow_size
    column_total = lax.psum(jnp.sum(clean_h, axis=0), ("wide", "narrow"))
    summary = jax.nn.sigmoid(column_total / node_total)
    probe = jnp.dot(disc_weight, summary, precision=lax.Precision.HIGHEST)
    clean_score = jnp.dot(clean_h, probe, precision=lax.Precision.HIGHEST)
    corrupt_score = jnp.dot(corrupt_h, probe, precision=lax.Precision.HIGHEST)
    local_terms = jnp.sum(jax.nn.softplus(-clean_score)) + jnp.sum(jax.nn.softplus(corrupt_score))
    loss = lax.psum(local_terms, ("wide", "narrow")) / (2 * node_total)
    return (clean_h.astype(jnp.bfloat16), jnp.stack((clean_score, corrupt_score)), loss)


def solution(mesh):
    placed = (
        P(("wide", "narrow"), None),
        P(),
        P(),
        P(),
        P("wide", "narrow", None, None, None),
        P("wide", "narrow", None),
        P("wide", "narrow", None),
        P("wide", "narrow"),
        P(),
        P(),
    )
    return jax.shard_map(
        shards,
        mesh=mesh,
        in_specs=placed,
        out_specs=(P(("wide", "narrow"), None), P(None, ("wide", "narrow")), P()),
        check_vma=False,
    )
```

profile of v0, /device:TPU:1, one launch (start us, length us, event | category | flops | bytes accessed | tf_op | source)
XLA Modules:
  0.0 729.2 jit_solution(8691298326891454932)
XLA Ops:
  12.4 4.5 fusion.7
  16.9 88.1 %all-gather.2.cloned.1.call-done = bf16[4096,768]{1,0:T(8,128)(2,1)} async-done(((bf16[256,768]{1,0:T(8,128)(2,1)}), bf16[4096,768]{1,0:T(8,128)(2,1)}) %all-gather.2.cloned.1.call-update) | async-done | bytes 6291472 | tf_op jit(solution)/shard_map/all_gather | solution.py:30
  105.0 7.8 %convolution_convert_fusion = bf16[4096,512]{1,0:T(8,128)(2,1)} fusion(bf16[4096,768]{1,0:T(8,128)(2,1)} %all-gather.2.cloned.1.call-done, bf16[768,512]{1,0:T(8,128)(2,1)S(1)} %copy-done.6), kind=kOutput, calls=%fused_computation.17 | convolution fusion | flops 3223322624 | bytes 11272192 | tf_op jit(solution)/shard_map/dot_general | solution.py:29
  112.8 4.9 gather_fusion.3
  117.8 4.6 broadcast_select_fusion
  122.4 7.9 %pad_maximum_fusion = bf16[16,256,1024]{2,1,0:T(8,128)(2,1)} fusion(bf16[16,256,512]{2,1,0:T(8,128)(2,1)} %broadcast_select_fusion, bf16[16,256,512]{2,1,0:T(8,128)(2,1)} %bitcast.86), kind=kLoop, calls=%fused_computation.13 | loop fusion | flops 16777216 | bytes 16777216 | tf_op jit(solution)/shard_map/concatenate | solution.py:57
  130.3 7.9 %broadcast_in_dim.15 = f32[16,256,1024]{2,1,0:T(8,128)} broadcast(f32[]{:T(128)} %constant.146.clone.1), dimensions={} | broadcast | bytes 16777220 | tf_op jit(solution)/shard_map/broadcast_in_dim | solution.py:65
  138.2 236.4 %while.11 = (s32[]{:T(128)}, f32[16,256,1024]{2,1,0:T(8,128)}, s32[]{:T(128)}, s32[24]{0:T(128)S(1)}, bf16[24,256,256]{2,1,0:T(8,128)(2,1)}, /*index=5*/s32[24]{...) while((s32[]{:T(128)}, f32[16,256,1024]{2,1,0:T(8,128)}, ...), condition=%wide.region_2.3_spmd, body=%wide.region_0.2_spmd.sunk | while | flops 134742048 | bytes 2753824 | solution.py:64
  154.4 3.4 fusion.43
  164.3 3.5 fusion.43
  174.2 3.4 fusion.43
  184.0 3.4 fusion.43
  193.8 3.4 fusion.43
  203.6 3.4 fusion.43
  223.3 3.4 fusion.43
  233.1 3.4 fusion.43
  243.0 3.4 fusion.43
  252.8 3.4 fusion.43
  282.2 3.4 fusion.43
  292.1 3.4 fusion.43
  321.5 3.4 fusion.43
  375.6 186.8 %reduce-scatter.2.cloned.1.call-done = f32[256,1024]{1,0:T(8,128)} async-done(((f32[4096,1024]{1,0:T(8,128)}), f32[256,1024]{1,0:T(8,128)}) %reduce-scatter.2.cloned.1.call-update) | async-done | bytes 1048592 | tf_op jit(solution)/shard_map/reduce_scatter | solution.py:67
  563.7 77.1 %psum.14 = f32[512]{0:T(512)S(1)} all-reduce(f32[512]{0:T(512)S(1)} %get-tuple-element.68), channel_id=1, replica_groups=mesh['wide'=16,'narrow'=16] {'wide','narrow'}, use_global_device_ids=true, to_apply=%region_5.6 | all-reduce | flops 512 | bytes 4096 | tf_op jit(solution)/shard_map/psum | solution.py:90
  648.0 72.6 %psum.15 = f32[]{:T(128)} all-reduce(f32[]{:T(128)S(6)} %add.223), channel_id=1, replica_groups=mesh['wide'=16,'narrow'=16] {'wide','narrow'}, use_global_device_ids=true, to_apply=%region_8.9 | all-reduce | flops 1 | bytes 8 | tf_op jit(solution)/shard_map/psum | solution.py:96
  (128 shorter events, 95.5 us)
Async XLA Ops:
  7.2 633.7 %copy-start = (f32[512,512]{1,0:T(8,128)S(1)}, f32[512,512]{1,0:T(8,128)}, u32[]{:S(2)}) copy-start(f32[512,512]{1,0:T(8,128)} %param.17) | copy-start | bytes 3145732
  7.2 97.8 %copy-start.6 = (bf16[768,512]{1,0:T(8,128)(2,1)S(1)}, bf16[768,512]{1,0:T(8,128)(2,1)}, u32[]{:S(2)}) copy-start(bf16[768,512]{1,0:T(8,128)(2,1)} %param.15) | copy-start | bytes 2359300
  7.2 97.8 %all-gather.2.cloned.1.call-start = ((), (), s32[]{:S(2)}) async-start(), calls=%async_computation.1 | async-start | bytes 6684672 | tf_op jit(solution)/shard_map/all_gather | solution.py:30
  7.9 554.5 %reduce-scatter.2.cloned.1.call-start = ((), (), s32[]{:S(2)}) async-start(), calls=%async_computation.2 | async-start | bytes 17825792 | tf_op jit(solution)/shard_map/reduce_scatter | solution.py:67
  130.3 7.9 %copy-start.2 = (s32[3]{0:T(128)S(1)}, s32[3]{0:T(128)}, u32[]{:S(2)}) copy-start(s32[3]{0:T(128)} %constant.143.clone.1) | copy-start | bytes 40
  130.3 7.9 %copy-start.4 = (s32[1,1,24]{2,1,0:T(1,128)S(1)}, s32[1,1,24]{2,1,0:T(1,128)}, u32[]{:S(2)}) copy-start(s32[1,1,24]{2,1,0:T(1,128)} %param.19) | copy-start | bytes 292
  130.3 7.9 %copy-start.5 = (s32[1,1,24]{2,1,0:T(1,128)S(1)}, s32[1,1,24]{2,1,0:T(1,128)}, u32[]{:S(2)}) copy-start(s32[1,1,24]{2,1,0:T(1,128)} %param.20) | copy-start | bytes 292
  374.6 1.0 copy-start.1
  374.6 187.8 %copy-start.3 = (f32[512]{0:T(512)S(1)}, f32[512]{0:T(512)}, u32[]{:S(2)}) copy-start(f32[512]{0:T(512)} %param.16) | copy-start | bytes 6148
Sparse Core Ops, SparseCore 0:
  10.5 94.4 all-gather.1
  374.7 187.6 reduce-scatter.1
where the time goes:
time: 732 us; the launch traced here: 729 us
  waiting for transfers between devices  276 us (38%)
  blocking collectives  150 us (20%)
  loops' own time  110 us (15%)
  matrix products  92.1 us (13%)
  local copies, waits for them, and re-layouts  44.7 us (6%)
  other arithmetic  39.8 us (5%)
  between operations  17.3 us (2%)
    reduce_scatter x1, waiting for transfers between devices, shards(): lax.psum_scatter(totals.reshape(tile_height * block_len, width), 'narrow'...  187 us
    another operation x1, loops' own time, shards(): lax.fori_loop(jnp.int32(0), live_slots, add_slot, jnp.zeros((tile_height,...  110 us
    all_gather x1, waiting for transfers between devices, shards(): lax.all_gather(features, 'wide', axis=0, tiled=True)  88.1 us
    dot_general x24, matrix products, add_slot(): jnp.dot(normed[slot], joined[slot_cols[slot]], preferred_element_type=jnp...  81.1 us
    psum x1, blocking collectives, shards(): column_total = lax.psum(jnp.sum(clean_h, axis=0), ('wide', 'narrow'))  77.1 us
    psum x1, blocking collectives, shards(): loss = lax.psum(local_terms, ('wide', 'narrow')) / (2 * node_total)  72.6 us
    another operation x24, other arithmetic  17.1 us
  transfers between devices with their start and end apart: 2, of which 2 were waited for; matrix products, arithmetic and copies ran while one was open for 1% of the time, Pallas kernels for 0%

commit v1 on v0

--- a/solution.py
+++ b/solution.py
@@ -87,7 +87,10 @@
         corrupt_sum + own_corrupt.astype(jnp.float32) / degree_float + bias, 0.0
     )
     node_total = rows_dev * wide_size * narrow_size
-    column_total = lax.psum(jnp.sum(clean_h, axis=0), ("wide", "narrow"))
+    pack_members_all_up = lambda frame_in, ax_name, dev_axis: jax.lax.psum(
+        jax.lax.psum(frame_in, ax_name), dev_axis
+    )
+    column_total = pack_members_all_up(jnp.sum(clean_h, axis=0), "narrow", "wide")
     summary = jax.nn.sigmoid(column_total / node_total)
     probe = jnp.dot(disc_weight, summary, precision=lax.Precision.HIGHEST)
     clean_score = jnp.dot(clean_h, probe, precision=lax.Precision.HIGHEST)

time: 732 us -> 728 us (level)
    psum x1 -> x2, blocking collectives: 77.1 us -> 65.9 us  [the longest x1 37.2 us: shards(): jax.lax.psum(jax.lax.psum(frame_in, ax_name), dev_axis)]
where the time goes in v1:
time: 728 us; the launch traced here: 725 us
  waiting for transfers between devices  276 us (38%)
  blocking collectives  145 us (20%)
  loops' own time  110 us (15%)
  matrix products  92.1 us (13%)
  local copies, waits for them, and re-layouts  44.7 us (6%)
  other arithmetic  39.8 us (5%)
  between operations  17.3 us (2%)
    reduce_scatter x1, waiting for transfers between devices, shards(): lax.psum_scatter(totals.reshape(tile_height * block_len, width), 'narrow'...  187 us
    another operation x1, loops' own time, shards(): lax.fori_loop(jnp.int32(0), live_slots, add_slot, jnp.zeros((tile_height,...  110 us
    all_gather x1, waiting for transfers between devices, shards(): lax.all_gather(features, 'wide', axis=0, tiled=True)  88.1 us
    dot_general x24, matrix products, add_slot(): jnp.dot(normed[slot], joined[slot_cols[slot]], preferred_element_type=jnp...  81.1 us
    psum x1, blocking collectives, shards(): loss = lax.psum(local_terms, ('wide', 'narrow')) / (2 * node_total)  79.3 us
    psum x1, blocking collectives, shards(): jax.lax.psum(jax.lax.psum(frame_in, ax_name), dev_axis)  37.2 us
    psum x1, blocking collectives, shards(): jax.lax.psum(frame_in, ax_name)  28.7 us
    another operation x24, other arithmetic  17.1 us
  transfers between devices with their start and end apart: 2, of which 2 were waited for; matrix products, arithmetic and copies ran while one was open for 1% of the time, Pallas kernels for 0%

profile of v1, /device:TPU:1, one launch (start us, length us, event | category | flops | bytes accessed | tf_op | source)
XLA Modules:
  0.0 724.7 jit_solution(17921881761844932424)
XLA Ops:
  12.4 4.5 fusion.7
  16.9 88.1 %all-gather.2.cloned.1.call-done = bf16[4096,768]{1,0:T(8,128)(2,1)} async-done(((bf16[256,768]{1,0:T(8,128)(2,1)}), bf16[4096,768]{1,0:T(8,128)(2,1)}) %all-gather.2.cloned.1.call-update) | async-done | bytes 6291472 | tf_op jit(solution)/shard_map/all_gather | solution.py:30
  105.0 7.8 %convolution_convert_fusion = bf16[4096,512]{1,0:T(8,128)(2,1)} fusion(bf16[4096,768]{1,0:T(8,128)(2,1)} %all-gather.2.cloned.1.call-done, bf16[768,512]{1,0:T(8,128)(2,1)S(1)} %copy-done.6), kind=kOutput, calls=%fused_computation.17 | convolution fusion | flops 3223322624 | bytes 11272192 | tf_op jit(solution)/shard_map/dot_general | solution.py:29
  112.8 4.9 gather_fusion.3
  117.8 4.6 broadcast_select_fusion
  122.4 7.9 %pad_maximum_fusion = bf16[16,256,1024]{2,1,0:T(8,128)(2,1)} fusion(bf16[16,256,512]{2,1,0:T(8,128)(2,1)} %broadcast_select_fusion, bf16[16,256,512]{2,1,0:T(8,128)(2,1)} %bitcast.86), kind=kLoop, calls=%fused_computation.13 | loop fusion | flops 16777216 | bytes 16777216 | tf_op jit(solution)/shard_map/concatenate | solution.py:57
  130.3 7.9 %broadcast_in_dim.15 = f32[16,256,1024]{2,1,0:T(8,128)} broadcast(f32[]{:T(128)} %constant.146.clone.1), dimensions={} | broadcast | bytes 16777220 | tf_op jit(solution)/shard_map/broadcast_in_dim | solution.py:65
  138.2 236.4 %while.11 = (s32[]{:T(128)}, f32[16,256,1024]{2,1,0:T(8,128)}, s32[]{:T(128)}, s32[24]{0:T(128)S(1)}, bf16[24,256,256]{2,1,0:T(8,128)(2,1)}, /*index=5*/s32[24]{...) while((s32[]{:T(128)}, f32[16,256,1024]{2,1,0:T(8,128)}, ...), condition=%wide.region_2.3_spmd, body=%wide.region_0.2_spmd.sunk | while | flops 134742048 | bytes 2753824 | solution.py:64
  154.4 3.4 fusion.43
  164.3 3.5 fusion.43
  174.2 3.4 fusion.43
  184.0 3.4 fusion.43
  193.8 3.4 fusion.43
  203.6 3.4 fusion.43
  223.3 3.4 fusion.43
  233.1 3.4 fusion.43
  243.0 3.4 fusion.43
  252.8 3.4 fusion.43
  292.1 3.4 fusion.43
  321.5 3.4 fusion.43
  375.6 186.8 %reduce-scatter.2.cloned.1.call-done = f32[256,1024]{1,0:T(8,128)} async-done(((f32[4096,1024]{1,0:T(8,128)}), f32[256,1024]{1,0:T(8,128)}) %reduce-scatter.2.cloned.1.call-update) | async-done | bytes 1048592 | tf_op jit(solution)/shard_map/reduce_scatter | solution.py:67
  563.7 28.7 %psum.21 = f32[512]{0:T(512)S(1)} all-reduce(f32[512]{0:T(512)S(1)} %get-tuple-element.68), channel_id=1, replica_groups=mesh['wide'=16,'narrow'=16] {'narrow'}, use_global_device_ids=true, to_apply=%region_5.6 | all-reduce | flops 512 | bytes 4096 | tf_op jit(solution)/shard_map/psum | solution.py:91
  592.4 37.2 %psum.22 = f32[512]{0:T(512)S(1)} all-reduce(f32[512]{0:T(512)S(1)} %psum.21), channel_id=1, replica_groups=mesh['wide'=16,'narrow'=16] {'wide'}, use_global_device_ids=true, to_apply=%region_6.7 | all-reduce | flops 512 | bytes 4096 | tf_op jit(solution)/shard_map/psum | solution.py:90
  636.8 79.3 %psum.23 = f32[]{:T(128)} all-reduce(f32[]{:T(128)S(6)} %add.225), channel_id=1, replica_groups=mesh['wide'=16,'narrow'=16] {'wide','narrow'}, use_global_device_ids=true, to_apply=%region_9.10 | all-reduce | flops 1 | bytes 8 | tf_op jit(solution)/shard_map/psum | solution.py:99
  (129 shorter events, 98.9 us)
Async XLA Ops:
  7.2 622.5 %copy-start = (f32[512,512]{1,0:T(8,128)S(1)}, f32[512,512]{1,0:T(8,128)}, u32[]{:S(2)}) copy-start(f32[512,512]{1,0:T(8,128)} %param.17) | copy-start | bytes 3145732
  7.2 97.8 %copy-start.6 = (bf16[768,512]{1,0:T(8,128)(2,1)S(1)}, bf16[768,512]{1,0:T(8,128)(2,1)}, u32[]{:S(2)}) copy-start(bf16[768,512]{1,0:T(8,128)(2,1)} %param.15) | copy-start | bytes 2359300
  7.2 97.8 %all-gather.2.cloned.1.call-start = ((), (), s32[]{:S(2)}) async-start(), calls=%async_computation.1 | async-start | bytes 6684672 | tf_op jit(solution)/shard_map/all_gather | solution.py:30
  7.9 554.5 %reduce-scatter.2.cloned.1.call-start = ((), (), s32[]{:S(2)}) async-start(), calls=%async_computation.2 | async-start | bytes 17825792 | tf_op jit(solution)/shard_map/reduce_scatter | solution.py:67
  130.3 7.9 %copy-start.2 = (s32[3]{0:T(128)S(1)}, s32[3]{0:T(128)}, u32[]{:S(2)}) copy-start(s32[3]{0:T(128)} %constant.143.clone.1) | copy-start | bytes 40
  130.3 7.9 %copy-start.4 = (s32[1,1,24]{2,1,0:T(1,128)S(1)}, s32[1,1,24]{2,1,0:T(1,128)}, u32[]{:S(2)}) copy-start(s32[1,1,24]{2,1,0:T(1,128)} %param.19) | copy-start | bytes 292
  130.3 7.9 %copy-start.5 = (s32[1,1,24]{2,1,0:T(1,128)S(1)}, s32[1,1,24]{2,1,0:T(1,128)}, u32[]{:S(2)}) copy-start(s32[1,1,24]{2,1,0:T(1,128)} %param.20) | copy-start | bytes 292
  374.6 1.0 copy-start.1
  374.6 187.8 %copy-start.3 = (f32[512]{0:T(512)S(1)}, f32[512]{0:T(512)}, u32[]{:S(2)}) copy-start(f32[512]{0:T(512)} %param.16) | copy-start | bytes 6148
Sparse Core Ops, SparseCore 0:
  10.5 94.4 all-gather.1
  374.7 187.6 reduce-scatter.1

commit v2 on v0

--- a/solution.py
+++ b/solution.py
@@ -2,6 +2,7 @@
 import jax.numpy as jnp
 from jax import lax
 from jax.sharding import PartitionSpec as P
+from jax.lax import all_gather
 
 
 def shards(
@@ -87,7 +88,9 @@
         corrupt_sum + own_corrupt.astype(jnp.float32) / degree_float + bias, 0.0
     )
     node_total = rows_dev * wide_size * narrow_size
-    column_total = lax.psum(jnp.sum(clean_h, axis=0), ("wide", "narrow"))
+    mine_x = jnp.sum(clean_h, axis=0)
+    t1 = all_gather(mine_x, axis_name=("wide", "narrow"))
+    column_total = jnp.sum(t1, 0)
     summary = jax.nn.sigmoid(column_total / node_total)
     probe = jnp.dot(disc_weight, summary, precision=lax.Precision.HIGHEST)
     clean_score = jnp.dot(clean_h, probe, precision=lax.Precision.HIGHEST)

time: 732 us -> 1000 us (1.37)
  blocking collectives: 150 us -> 420 us
    all_gather x0 -> x1, blocking collectives: none -> 348 us  [shards(): t1 = all_gather(mine_x, axis_name=('wide', 'narrow'))]
    psum x1 -> x0, blocking collectives: 77.1 us -> none  [shards(): column_total = lax.psum(jnp.sum(clean_h, axis=0), ('wide', 'narrow'))]
where the time goes in v2:
time: 1000 us
  blocking collectives  420 us (42%)
  waiting for transfers between devices  276 us (28%)
  loops' own time  110 us (11%)
  matrix products  92.1 us (9%)
  local copies, waits for them, and re-layouts  44.7 us (4%)
  other arithmetic  40.1 us (4%)
  between operations  17.3 us (2%)
    all_gather x1, blocking collectives, shards(): t1 = all_gather(mine_x, axis_name=('wide', 'narrow'))  348 us
    reduce_scatter x1, waiting for transfers between devices, shards(): lax.psum_scatter(totals.reshape(tile_height * block_len, width), 'narrow'...  187 us
    another operation x1, loops' own time, shards(): lax.fori_loop(jnp.int32(0), live_slots, add_slot, jnp.zeros((tile_height,...  110 us
    all_gather x1, waiting for transfers between devices, shards(): lax.all_gather(features, 'wide', axis=0, tiled=True)  88.1 us
    dot_general x24, matrix products, add_slot(): jnp.dot(normed[slot], joined[slot_cols[slot]], preferred_element_type=jnp...  81.1 us
    psum x1, blocking collectives, shards(): loss = lax.psum(local_terms, ('wide', 'narrow')) / (2 * node_total)  72.6 us
  transfers between devices with their start and end apart: 2, of which 2 were waited for; matrix products, arithmetic and copies ran while one was open for 1% of the time, Pallas kernels for 0%

profile of v2, /device:TPU:1, one launch (start us, length us, event | category | flops | bytes accessed | tf_op | source)
XLA Modules:
  0.0 999.9 jit_solution(1237543420022804788)
XLA Ops:
  12.4 4.5 fusion.7
  16.9 88.1 %all-gather.4.cloned.1.call-done = bf16[4096,768]{1,0:T(8,128)(2,1)} async-done(((bf16[256,768]{1,0:T(8,128)(2,1)}), bf16[4096,768]{1,0:T(8,128)(2,1)}) %all-gather.4.cloned.1.call-update) | async-done | bytes 6291472 | tf_op jit(solution)/shard_map/all_gather | solution.py:31
  105.0 7.8 convolution_convert_fusion
  112.8 4.9 gather_fusion.3
  117.8 4.6 broadcast_select_fusion
  122.4 7.9 pad_maximum_fusion
  130.3 7.9 broadcast_in_dim.15
  138.2 236.4 %while.11 = (s32[]{:T(128)}, f32[16,256,1024]{2,1,0:T(8,128)}, s32[]{:T(128)}, s32[24]{0:T(128)S(1)}, bf16[24,256,256]{2,1,0:T(8,128)(2,1)}, /*index=5*/s32[24]{...) while((s32[]{:T(128)}, f32[16,256,1024]{2,1,0:T(8,128)}, ...), condition=%wide.region_2.3_spmd, body=%wide.region_0.2_spmd.sunk | while | flops 134742048 | bytes 2753824 | solution.py:65
  154.4 3.4 fusion.43
  164.3 3.5 fusion.43
  174.2 3.4 fusion.43
  184.0 3.4 fusion.43
  193.8 3.4 fusion.43
  203.6 3.4 fusion.43
  223.3 3.4 fusion.43
  233.1 3.4 fusion.43
  243.0 3.4 fusion.43
  252.8 3.4 fusion.43
  282.2 3.4 fusion.43
  292.1 3.4 fusion.43
  321.5 3.4 fusion.43
  375.6 186.8 %reduce-scatter.2.cloned.1.call-done = f32[256,1024]{1,0:T(8,128)} async-done(((f32[4096,1024]{1,0:T(8,128)}), f32[256,1024]{1,0:T(8,128)}) %reduce-scatter.2.cloned.1.call-update) | async-done | bytes 1048592 | tf_op jit(solution)/shard_map/reduce_scatter | solution.py:68
  563.7 347.5 %all-gather.1 = f32[256,1,512]{2,1,0:T(1,128)S(1)} all-gather(f32[1,1,512]{2,1,0:T(1,128)S(1)} %bitcast.90), channel_id=2, replica_groups=mesh['wide'=16,'narrow'=16] {'wide','narrow'}, dimensions={0}, use_global_device_ids=true | all-gather | bytes 526336 | tf_op jit(solution)/shard_map/all_gather | solution.py:92
  918.7 72.6 %psum.7 = f32[]{:T(128)} all-reduce(f32[]{:T(128)S(6)} %add.221), channel_id=1, replica_groups=mesh['wide'=16,'narrow'=16] {'wide','narrow'}, use_global_device_ids=true, to_apply=%region_8.9 | all-reduce | flops 1 | bytes 8 | tf_op jit(solution)/shard_map/psum | solution.py:99
  (129 shorter events, 95.9 us)
Async XLA Ops:
  7.2 904.4 %copy-start = (f32[512,512]{1,0:T(8,128)S(1)}, f32[512,512]{1,0:T(8,128)}, u32[]{:S(2)}) copy-start(f32[512,512]{1,0:T(8,128)} %param.17) | copy-start | bytes 3145732
  7.2 97.8 %copy-start.6 = (bf16[768,512]{1,0:T(8,128)(2,1)S(1)}, bf16[768,512]{1,0:T(8,128)(2,1)}, u32[]{:S(2)}) copy-start(bf16[768,512]{1,0:T(8,128)(2,1)} %param.15) | copy-start | bytes 2359300
  7.2 97.8 %all-gather.4.cloned.1.call-start = ((), (), s32[]{:S(2)}) async-start(), calls=%async_computation.1 | async-start | bytes 6684672 | tf_op jit(solution)/shard_map/all_gather | solution.py:31
  7.9 554.5 %reduce-scatter.2.cloned.1.call-start = ((), (), s32[]{:S(2)}) async-start(), calls=%async_computation.2 | async-start | bytes 17825792 | tf_op jit(solution)/shard_map/reduce_scatter | solution.py:68
  130.3 7.9 copy-start.2
  130.3 7.9 copy-start.4
  130.3 7.9 copy-start.5
  374.6 1.0 copy-start.1
  374.6 187.8 %copy-start.3 = (f32[512]{0:T(512)S(1)}, f32[512]{0:T(512)}, u32[]{:S(2)}) copy-start(f32[512]{0:T(512)} %param.16) | copy-start | bytes 6148
Sparse Core Ops, SparseCore 0:
  10.5 94.4 all-gather.3
  374.7 187.6 reduce-scatter.1
